TPU v7x, 32 devices: a whole 2x2x4 slice. The times are simulated.
32 devices in a mesh: sector: 16 (over z, y, x), dof: 2 (over core).
Axes of the slice: x: 2, y: 2, z: 4, core: 2. Of those that a mesh axis runs over, the one named last changes fastest.
Arguments:
- loads: bfloat16 [16, 128, 32768], P('sector', None, 'dof'), may hold values from -0.75 to 0.75
- modes: bfloat16 [32768, 512], P('dof'), may hold values from -0.25 to 0.25
- response: float32 [16, 128, 512], P('sector', None, 'dof'), may hold values from -6 to 6
- pattern: int32 [16], P('sector'), may hold values from 0 to 7
- deviation: float32 [8, 512], replicated, may hold values from -1 to 1
- eigen: float32 [16, 512], replicated, may hold values from 1 to 10
- loss: float32 [512], replicated, may hold values from 0.2 to 0.6
- omega_sq: float32 [64], replicated, may hold values from 0.5 to 12
- iface_left: int32 [1024], P('dof'), may hold values from 0 to 16383, as said below
- iface_right: int32 [1024], P('dof'), may hold values from 0 to 16383, as said below
Outputs:
- modal_response: float32 [16, 128, 512], P('sector', None, 'dof')
- displacement: bfloat16 [16, 128, 32768], P('sector', None, 'dof')
Inputs may be any that keep to these rules, and one draw needn't show every extreme that they name: Within each block of 512 entries, the entries of iface_left and of iface_right together are (2) * 512 distinct rows. `iface_right`: see iface_left.
All inputs are finite; a program needn't handle non-finite values.
Results may differ from a plain program's by a relative error of at most 0.005.
Values may be sent and summed in bfloat16 or wider, within the bound.
A program may use at most 128 MiB of HBM per device.

v0:
```python
import math
import jax
import jax.numpy as jnp
from jax import lax
from jax.sharding import PartitionSpec as P


def shifted_2(shard, axis, by):
    size = lax.axis_size(axis)
    return lax.ppermute(shard, axis, [(i, (i + by) % size) for i in range(size)])


def tables(row_count, col_count, sectors):
    rows_idx = jnp.arange(row_count, dtype=jnp.int32) % sectors
    cols_idx = jnp.arange(col_count, dtype=jnp.int32) % sectors
    turns = rows_idx[:, None] * cols_idx[None, :] % sectors
    theta = turns.astype(jnp.float32) * (2.0 * math.pi / sectors)
    return (jnp.cos(theta), jnp.sin(theta))


def divide(spec_re, spec_im, shifted, damped):
    denom = shifted * shifted + damped * damped
    return (
        (spec_re * shifted + spec_im * damped) / denom,
        (spec_im * shifted - spec_re * damped) / denom,
    )


def shards(
    loads, modes, response, pattern, deviation, eigen, loss, omega_sq, iface_left, iface_right
):
    highest = lax.Precision.HIGHEST
    local_sec, rows_two, dof_rows = loads.shape
    freqs = rows_two // 2
    modes_all = modes.shape[1]
    sec_devices = lax.axis_size("sector")
    sectors = sec_devices * local_sec
    half = modes_all // lax.axis_size("dof")
    width = freqs * half
    first_mode = lax.axis_index("dof") * half
    partial_force = jnp.dot(
        loads.reshape(local_sec * rows_two, dof_rows), modes, preferred_element_type=jnp.float32
    )
    force = lax.psum_scatter(
        partial_force.reshape(local_sec, rows_two, modes_all),
        "dof",
        scatter_dimension=2,
        tiled=True,
    )
    table_count = deviation.shape[0]
    dev_half = lax.dynamic_slice_in_dim(deviation, first_mode, half, 1)
    onehot = (pattern[:, None] == jnp.arange(table_count, dtype=jnp.int32)[None, :]).astype(
        jnp.float32
    )
    dev_rows = jnp.dot(onehot, dev_half, precision=highest)
    rest = (force - dev_rows[:, None, :] * response).reshape(local_sec, 2, width)
    columns = lax.all_to_all(rest, "sector", split_axis=2, concat_axis=0, tiled=True)
    share = width // sec_devices
    col_idx = lax.axis_index("sector") * share + jnp.arange(share, dtype=jnp.int32)
    freq_idx = col_idx // half
    mode_idx = first_mode + col_idx % half
    stiff = jnp.take(eigen, mode_idx, axis=1)
    shifted = stiff - jnp.take(omega_sq, freq_idx)[None, :]
    damped = jnp.take(loss, mode_idx)[None, :] * stiff
    cosine, sine = tables(sectors, sectors, sectors)
    spec_re = jnp.dot(cosine, columns[:, 0], precision=highest) + jnp.dot(
        sine, columns[:, 1], precision=highest
    )
    spec_im = jnp.dot(cosine, columns[:, 1], precision=highest) - jnp.dot(
        sine, columns[:, 0], precision=highest
    )
    solved_re, solved_im = divide(spec_re, spec_im, shifted, damped)
    out_re = (
        jnp.dot(cosine, solved_re, precision=highest) - jnp.dot(sine, solved_im, precision=highest)
    ) / sectors
    out_im = (
        jnp.dot(cosine, solved_im, precision=highest) + jnp.dot(sine, solved_re, precision=highest)
    ) / sectors
    updated = lax.all_to_all(
        jnp.stack([out_re, out_im], 1).astype(jnp.bfloat16),
        "sector",
        split_axis=0,
        concat_axis=2,
        tiled=True,
    ).astype(jnp.float32)
    modal_response = updated.reshape(local_sec, rows_two, half)
    rounded = modal_response.astype(jnp.bfloat16)
    raw = jnp.einsum(
        "skm,dm->skd",
        lax.all_gather(rounded, "dof", axis=2, tiled=True),
        modes,
        preferred_element_type=jnp.float32,
    ).astype(jnp.bfloat16)
    left_vals = jnp.take(raw, iface_left, axis=2)
    right_vals = jnp.take(raw, iface_right, axis=2)
    next_left = shifted_2(left_vals, "sector", -1)
    prev_right = shifted_2(right_vals, "sector", 1)
    left_after = jnp.concatenate([left_vals[1:], next_left], 0)
    right_before = jnp.concatenate([prev_right, right_vals[:-1]], 0)
    right_new = (0.5 * (right_vals.astype(jnp.float32) + left_after.astype(jnp.float32))).astype(
        jnp.bfloat16
    )
    left_new = (0.5 * (right_before.astype(jnp.float32) + left_vals.astype(jnp.float32))).astype(
        jnp.bfloat16
    )
    displacement = raw.at[:, :, iface_right].set(right_new).at[:, :, iface_left].set(left_new)
    return (modal_response, displacement)


def solution(mesh):
    placed = (
        P("sector", None, "dof"),
        P("dof", None),
        P("sector", None, "dof"),
        P("sector"),
        P(),
        P(),
        P(),
        P(),
        P("dof"),
        P("dof"),
    )
    return jax.shard_map(
        shards,
        mesh=mesh,
        in_specs=placed,
        out_specs=(P("sector", None, "dof"), P("sector", None, "dof")),
        check_vma=False,
    )
```

profile of v0, /device:TPU:0, one launch (start us, length us, event | category | flops | bytes accessed | tf_op | source)
XLA Modules:
  0.0 273.0 jit_solution(13463132247253687220)
XLA Ops:
  7.3 10.1 %fusion.2 = f32[1,128,512]{2,1,0:T(8,128)} fusion(bf16[16384,512]{1,0:T(8,128)(2,1)} %param.13, bf16[1,128,16384]{2,1,0:T(8,128)(2,1)} %param.12), kind=kOutput, calls=%fused_computation.9 | convolution fusion | flops 2147483648 | bytes 21233664 | tf_op jit(solution)/shard_map/dot_general | solution.py:41
  19.0 0.7 fusion.90
  19.8 0.7 fusion.91
  20.4 0.7 fusion.88
  21.2 0.7 fusion.89
  22.7 6.9 %gather_fusion.1 = f32[1024]{0:T(1024)S(1)} fusion(f32[512]{0:T(512)S(1)} %copy-done.1, s32[1024]{0:T(1024)S(1)} %broadcast_clamp_fusion), kind=kCustom, calls=%fused_computation.3 | custom fusion | bytes 12288 | tf_op jit(solution)/shard_map/jit(_take)/gather | solution.py:64
  29.7 4.4 %compare_select_fusion.2 = f32[1024,1]{0,1:T(1,128)S(1)} fusion(f32[]{:T(128)} %bitcast.69, f32[]{:T(128)} %bitcast.70, f32[]{:T(128)} %bitcast.71, f32[]{:T(128)} %bitcast.72, f32[]{:T(128)} %bitcast.73, f32[]{:T(128)} %bitcast.75, f32[]{:T(128)} %bitcast.74, s32[]{:T(128)S(6)} %mul.129), kind=kLoop, calls=%fused_computation.107 | loop fusion | flops 31744 | bytes 4128 | tf_op jit(solution)/shard_map/jit(_take)/gather | solution.py:63
  34.1 0.9 multiply_subtract_fusion
  35.1 12.0 %copy.32 = f32[1,2,16384]{1,0,2:T(1,128)} copy(f32[1,2,16384]{2,1,0:T(2,128)S(1)} %reshape.256) | data formatting | bytes 262144 | tf_op jit(solution)/shard_map/reshape | solution.py:56
  47.2 0.5 broadcast.1041
  47.7 74.5 %reduce.114 = f32[16384,2]{1,0:T(8,128)} reduce(f32[16384,1,2]{2,1,0:T(1,128)} %bitcast.171, f32[]{:T(128)} %broadcast.1041), dimensions={1}, to_apply=%bitcast.154.reduce_sub_computation | reduce | bytes 262148
  122.1 8.2 %reshape.603 = f32[16,1,2048]{2,1,0:T(1,128)} reshape(f32[16384,2]{1,0:T(8,128)} %reduce.114) | data formatting | bytes 262144
  130.4 8.4 %all-to-all-start = ((f32[16,1,2048]{2,1,0:T(1,128)}), f32[16,1,2048]{2,1,0:T(1,128)S(1)}, u32[]{:S(2)}, u32[]{:S(2)}) async-start(f32[16,1,2048]{2,1,0:T(1,128)} %reshape.603), calls=%async_computation.1 | async-start | bytes 262144 | tf_op jit(solution)/shard_map/all_to_all | solution.py:57
  138.9 2.8 %gather_fusion = f32[1024,16]{1,0:T(8,128)S(1)} fusion(f32[16,512]{0,1:T(8,128)S(1)} %copy.34, s32[1024]{0:T(1024)S(1)} %broadcast_clamp_fusion), kind=kCustom, calls=%fused_computation.2 | custom fusion | bytes 135168 | tf_op jit(solution)/shard_map/jit(_take)/gather | solution.py:62
  142.0 35.5 %select_select_fusion = f32[1024]{0:T(1024)S(1)} fusion(pred[1024]{0:T(1024)(128)(4,1)S(1)} %get-tuple-element.77, pred[1024]{0:T(1024)(128)(4,1)S(1)} %get-tuple-element.78, pred[1024]{0:T(1024)(128)(4,1)S(1)} %get-tuple-element.79, pred[1024]{0:T(1024)(128)(4,1)S(1)} %get-tuple-element.80, pred[1024]{0:T(1024)(128)(4,1)S(1)} %get-tuple-element.81, ...), kind=kLoop, calls=%fused_computation.141 | loop fusion | flops 81920 | bytes 66792 | tf_op jit(solution)/shard_map/jit(_take)/select_n | solution.py:63
  177.6 1.0 reduce.115
  178.5 14.7 %reshape.604 = f32[16384,1,2]{2,1,0:T(1,128)} reshape(f32[16,2048]{1,0:T(8,128)S(1)} %reduce.115) | data formatting | bytes 262144
  193.3 5.2 %copy.42 = f32[1,2,16,1024]{3,2,1,0:T(8,128)S(1)} copy(f32[1,2,16,1024]{1,3,2,0:T(8,128)} %bitcast.172) | data formatting | bytes 262144 | tf_op jit(solution)/shard_map/all_to_all | solution.py:57
  201.1 0.7 copy.36
  201.8 6.9 %all-to-all-start.1 = ((bf16[16,2,1024]{2,1,0:T(2,128)(2,1)}), bf16[16,2,1024]{2,1,0:T(2,128)(2,1)S(1)}, u32[]{:S(2)}, u32[]{:S(2)}) async-start(bf16[16,2,1024]{2,1,0:T(2,128)(2,1)} %copy.36), calls=%async_computation.2 | async-start | bytes 131072 | tf_op jit(solution)/shard_map/all_to_all | solution.py:79
  208.7 7.5 %all-to-all-done.1 = bf16[16,2,1024]{2,1,0:T(2,128)(2,1)S(1)} async-done(((bf16[16,2,1024]{2,1,0:T(2,128)(2,1)}), bf16[16,2,1024]{2,1,0:T(2,128)(2,1)S(1)}, u32[]{:S(2)}, u32[]{:S(2)}) %all-to-all-start.1) | async-done | bytes 65568 | tf_op jit(solution)/shard_map/all_to_all | solution.py:79
  216.3 1.9 all_gather.3
  218.2 10.3 %convolution_convert_fusion = bf16[128,16384]{1,0:T(8,128)(2,1)} fusion(bf16[16384,512]{1,0:T(8,128)(2,1)} %param.13, bf16[1,128,512]{2,1,0:T(8,128)(2,1)S(1)} %all_gather.3), kind=kOutput, calls=%fused_computation.6 | convolution fusion | flops 2149580800 | bytes 21102592 | tf_op jit(solution)/shard_map/skm,dm->skd/dot_general | solution.py:88
  228.6 6.4 %copy.40 = bf16[128,16384]{0,1:T(8,128)(2,1)} copy(bf16[128,16384]{1,0:T(8,128)(2,1)} %convolution_convert_fusion) | data formatting | bytes 8388608 | tf_op jit(solution)/shard_map/convert_element_type | solution.py:93
  235.0 3.8 %gather_fusion.3 = bf16[512,128]{1,0:T(8,128)(2,1)S(1)} fusion(bf16[128,16384]{0,1:T(8,128)(2,1)} %copy.40, s32[1024]{0:T(1024)S(1)} %pad_clamp_fusion), kind=kCustom, calls=%fused_computation.1.clone | custom fusion | bytes 264192 | tf_op jit(solution)/shard_map/jit(_take)/gather | solution.py:94
  238.9 1.0 collective-permute-start
  239.9 3.8 %gather_fusion.2 = bf16[512,128]{1,0:T(8,128)(2,1)S(1)} fusion(bf16[128,16384]{0,1:T(8,128)(2,1)} %copy.40, s32[1024]{0:T(1024)S(1)} %pad_clamp_fusion.1), kind=kCustom, calls=%fused_computation.clone | custom fusion | bytes 264192 | tf_op jit(solution)/shard_map/jit(_take)/gather | solution.py:95
  243.8 1.3 collective-permute-start.1
  245.2 0.7 convert_element_type.61
  245.8 6.8 %scatter_custom_fusion = bf16[128,16384]{0,1:T(8,128)(2,1)} fusion(bf16[128,16384]{0,1:T(8,128)(2,1)} %copy.40, s32[512]{0:T(512)S(1)} %compare_select_fusion.14, bf16[1,128,512]{1,2,0:T(8,128)(2,1)S(1)} %collective-permute-done, f32[]{:T(128)} %constant.134.clone.1, bf16[512,128]{1,0:T(8,128)(2,1)S(1)} %gather_fusion.2, ...), kind=kCustom, calls=%fused_computation.23 | custom fusion | flops 393216 | bytes 4457472 | tf_op jit(solution)/shard_map/scatter | solution.py:106
  253.0 6.8 %scatter_custom_fusion.1 = bf16[128,16384]{0,1:T(8,128)(2,1)} fusion(bf16[128,16384]{0,1:T(8,128)(2,1)} %scatter_custom_fusion, s32[512]{0:T(512)S(1)} %compare_select_fusion.13, bf16[1,128,512]{1,2,0:T(8,128)(2,1)S(1)} %collective-permute-done.1, f32[]{:T(128)} %constant.134.clone.1, bf16[512,128]{1,0:T(8,128)(2,1)S(1)} %gather_fusion.3, ...), kind=kCustom, calls=%fused_computation.25 | custom fusion | flops 393216 | bytes 4457472 | tf_op jit(solution)/shard_map/scatter | solution.py:106
  259.8 6.4 %copy.41 = bf16[1,128,16384]{2,1,0:T(8,128)(2,1)} copy(bf16[1,128,16384]{1,2,0:T(8,128)(2,1)} %bitcast.173) | data formatting | bytes 8388608
  (77 shorter events, 5.6 us)
Async XLA Ops:
  7.2 22.4 %copy-start = (f32[8,512]{1,0:T(8,128)S(1)}, f32[8,512]{1,0:T(8,128)}, u32[]{:S(2)}) copy-start(f32[8,512]{1,0:T(8,128)} %param.16) | copy-start | bytes 49156
  7.2 11.8 %copy-start.2 = (f32[64]{0:T(128)S(1)}, f32[64]{0:T(128)}, u32[]{:S(2)}) copy-start(f32[64]{0:T(128)} %param.19) | copy-start | bytes 772
  7.2 14.7 %copy-start.5 = (s32[512]{0:T(512)S(1)}, s32[512]{0:T(512)}, u32[]{:S(2)}) copy-start(s32[512]{0:T(512)} %param.21) | copy-start | bytes 6148
  7.2 15.4 %copy-start.6 = (s32[512]{0:T(512)S(1)}, s32[512]{0:T(512)}, u32[]{:S(2)}) copy-start(s32[512]{0:T(512)} %param.20) | copy-start | bytes 6148
  7.2 15.4 %copy-start.1 = (f32[512]{0:T(512)S(1)}, f32[512]{0:T(512)}, u32[]{:S(2)}) copy-start(f32[512]{0:T(512)} %param.18) | copy-start | bytes 6148
  7.2 26.9 %reduce-scatter.2.cloned.1.call-start = ((), (), s32[]{:S(2)}) async-start(), calls=%async_computation.3 | async-start | bytes 393216 | tf_op jit(solution)/shard_map/reduce_scatter | solution.py:44
  17.4 16.8 %copy-start.3 = (f32[1,128,256]{2,1,0:T(8,128)S(1)}, f32[1,128,256]{2,1,0:T(8,128)}, u32[]{:S(2)}) copy-start(f32[1,128,256]{2,1,0:T(8,128)} %param.14) | copy-start | bytes 393220
  122.1 16.6 %copy-start.4 = (f32[16,512]{1,0:T(8,128)S(1)}, f32[16,512]{1,0:T(8,128)}, u32[]{:S(2)}) copy-start(f32[16,512]{1,0:T(8,128)} %param.17) | copy-start | bytes 98308
  130.4 47.2 %all-to-all-start = ((f32[16,1,2048]{2,1,0:T(1,128)}), f32[16,1,2048]{2,1,0:T(1,128)S(1)}, u32[]{:S(2)}, u32[]{:S(2)}) async-start(f32[16,1,2048]{2,1,0:T(1,128)} %reshape.603), calls=%async_computation.1 | async-start | bytes 262144 | tf_op jit(solution)/shard_map/all_to_all | solution.py:57
  201.8 14.4 %all-to-all-start.1 = ((bf16[16,2,1024]{2,1,0:T(2,128)(2,1)}), bf16[16,2,1024]{2,1,0:T(2,128)(2,1)S(1)}, u32[]{:S(2)}, u32[]{:S(2)}) async-start(bf16[16,2,1024]{2,1,0:T(2,128)(2,1)} %copy.36), calls=%async_computation.2 | async-start | bytes 131072 | tf_op jit(solution)/shard_map/all_to_all | solution.py:79
  238.9 7.0 %collective-permute-start = (bf16[1,128,512]{1,2,0:T(8,128)(2,1)S(1)}, bf16[1,128,512]{1,2,0:T(8,128)(2,1)S(1)}, u32[]{:S(2)}, u32[]{:S(2)}) collective-permute-start(bf16[1,128,512]{1,2,0:T(8,128)(2,1)S(1)} %bitcast_select_fusion), channel_id=1, source_target_pairs={{0,30},{2,0},{4,2},{6,4},{8,6},{10,8},{12,10},{14,12},{16,14},{18,... | collective-permute-start | bytes 393224 | tf_op jit(solution)/shard_map/ppermute | solution.py:10
  243.8 9.1 %collective-permute-start.1 = (bf16[1,128,512]{1,2,0:T(8,128)(2,1)S(1)}, bf16[1,128,512]{1,2,0:T(8,128)(2,1)S(1)}, u32[]{:S(2)}, u32[]{:S(2)}) collective-permute-start(bf16[1,128,512]{1,2,0:T(8,128)(2,1)S(1)} %bitcast_select_fusion.1), channel_id=1, source_target_pairs={{0,2},{2,4},{4,6},{6,8},{8,10},{10,12},{12,14},{14,16},{16,18},{18... | collective-permute-start | bytes 393224 | tf_op jit(solution)/shard_map/ppermute | solution.py:10
Sparse Core Ops, SparseCore 0:
  17.5 10.4 reduce-scatter.1
where the time goes:
time: 274 us; the launch traced here: 273 us
  other arithmetic  133 us (49%)
  local copies, waits for them, and re-layouts  74.7 us (27%)
  matrix products  23.1 us (8%)
  starting transfers between devices  17.6 us (6%)
  between operations  15.1 us (6%)
  waiting for transfers between devices  7.82 us (3%)
    unnamed x1, other arithmetic  74.5 us
    select_n x1, other arithmetic, shards(): shifted = stiff - jnp.take(omega_sq, freq_idx)[None, :]  35.5 us
    unnamed x19, local copies, waits for them, and re-layouts  30 us
    scatter x2, other arithmetic, shards(): raw.at[:, :, iface_right].set(right_new).at[:, :, iface_left].set(left_new)  13.7 us
    reshape x2, local copies, waits for them, and re-layouts, shards(): (force - dev_rows[:, None, :] * response).reshape(local_sec, 2, width)  12.1 us
    dot_general x1, matrix products, shards(): jnp.einsum('skm,dm->skd', lax.all_gather(rounded, 'dof', axis=2, tiled=Tr...  10.3 us
    dot_general x1, matrix products, shards(): jnp.dot(loads.reshape(local_sec * rows_two, dof_rows), modes, preferred_e...  10.1 us
    all_to_all x1, starting transfers between devices, shards(): lax.all_to_all(rest, 'sector', split_axis=2, concat_axis=0, tiled=True)  8.35 us
  transfers between devices with their start and end apart: 5, of which 2 were waited for; matrix products, arithmetic and copies ran while one was open for 24% of the time, Pallas kernels for 0%

commit v1 on v0

--- a/solution.py
+++ b/solution.py
@@ -76,12 +76,20 @@
     out_im = (
         jnp.dot(cosine, solved_im, precision=highest) + jnp.dot(sine, solved_re, precision=highest)
     ) / sectors
-    updated = lax.all_to_all(
-        jnp.stack([out_re, out_im], 1).astype(jnp.bfloat16),
-        "sector",
-        split_axis=0,
-        concat_axis=2,
-        tiled=True,
+    updated = jnp.concatenate(
+        lax.all_to_all(
+            jnp.stack(
+                jnp.split(
+                    jnp.stack([out_re, out_im], 1).astype(jnp.bfloat16),
+                    lax.axis_size("sector"),
+                    axis=0,
+                )
+            ),
+            "sector",
+            0,
+            0,
+        ),
+        axis=2,
     ).astype(jnp.float32)
     modal_response = updated.reshape(local_sec, rows_two, half)
     rounded = modal_response.astype(jnp.bfloat16)

time: 274 us -> 283 us (1.033)
  local copies, waits for them, and re-layouts: 74.7 us -> 83.6 us
    unnamed x19 -> x34, local copies, waits for them, and re-layouts: 30 us -> 39 us
  transfers between devices with their start and end apart: 5 -> 5, of which waited for: 2 -> 2; matrix products, arithmetic and copies ran while one was open for 24% -> 23% of each run, Pallas kernels for 0% -> 0%
where the time goes in v1:
time: 283 us; the launch traced here: 282 us
  other arithmetic  133 us (47%)
  local copies, waits for them, and re-layouts  83.6 us (30%)
  matrix products  23.1 us (8%)
  starting transfers between devices  17.6 us (6%)
  between operations  15.1 us (5%)
  waiting for transfers between devices  7.83 us (3%)
    unnamed x1, other arithmetic  74.5 us
    unnamed x34, local copies, waits for them, and re-layouts  39 us
    select_n x1, other arithmetic, shards(): shifted = stiff - jnp.take(omega_sq, freq_idx)[None, :]  35.5 us
    scatter x2, other arithmetic, shards(): raw.at[:, :, iface_right].set(right_new).at[:, :, iface_left].set(left_new)  13.7 us
    reshape x2, local copies, waits for them, and re-layouts, shards(): (force - dev_rows[:, None, :] * response).reshape(local_sec, 2, width)  12.1 us
    dot_general x1, matrix products, shards(): jnp.einsum('skm,dm->skd', lax.all_gather(rounded, 'dof', axis=2, tiled=Tr...  10.3 us
    dot_general x1, matrix products, shards(): jnp.dot(loads.reshape(local_sec * rows_two, dof_rows), modes, preferred_e...  10.1 us
    all_to_all x1, starting transfers between devices, shards(): lax.all_to_all(rest, 'sector', split_axis=2, concat_axis=0, tiled=True)  8.35 us
  transfers between devices with their start and end apart: 5, of which 2 were waited for; matrix products, arithmetic and copies ran while one was open for 23% of the time, Pallas kernels for 0%

profile of v1, /device:TPU:0, one launch (start us, length us, event | category | flops | bytes accessed | tf_op | source)
XLA Modules:
  0.0 282.0 jit_solution(8127292639535505862)
XLA Ops:
  7.3 10.1 %fusion.2 = f32[1,128,512]{2,1,0:T(8,128)} fusion(bf16[16384,512]{1,0:T(8,128)(2,1)} %param.13, bf16[1,128,16384]{2,1,0:T(8,128)(2,1)} %param.12), kind=kOutput, calls=%fused_computation.9 | convolution fusion | flops 2147483648 | bytes 21233664 | tf_op jit(solution)/shard_map/dot_general | solution.py:41
  19.0 0.7 fusion.105
  19.7 0.7 fusion.106
  20.4 0.7 fusion.103
  21.2 0.7 fusion.104
  22.6 6.9 %gather_fusion.1 = f32[1024]{0:T(1024)S(1)} fusion(f32[512]{0:T(512)S(1)} %copy-done.1, s32[1024]{0:T(1024)S(1)} %broadcast_clamp_fusion), kind=kCustom, calls=%fused_computation.3 | custom fusion | bytes 12288 | tf_op jit(solution)/shard_map/jit(_take)/gather | solution.py:64
  29.6 4.4 %compare_select_fusion.2 = f32[1024,1]{0,1:T(1,128)S(1)} fusion(f32[]{:T(128)} %bitcast.69, f32[]{:T(128)} %bitcast.70, f32[]{:T(128)} %bitcast.71, f32[]{:T(128)} %bitcast.72, f32[]{:T(128)} %bitcast.73, f32[]{:T(128)} %bitcast.75, f32[]{:T(128)} %bitcast.74, s32[]{:T(128)S(6)} %mul.129), kind=kLoop, calls=%fused_computation.152 | loop fusion | flops 31744 | bytes 4128 | tf_op jit(solution)/shard_map/jit(_take)/gather | solution.py:63
  34.1 0.9 multiply_subtract_fusion
  35.1 12.0 %copy.258 = f32[1,2,16384]{1,0,2:T(1,128)} copy(f32[1,2,16384]{2,1,0:T(2,128)S(1)} %reshape.262) | data formatting | bytes 262144 | tf_op jit(solution)/shard_map/reshape | solution.py:56
  47.7 74.5 %reduce.114 = f32[16384,2]{1,0:T(8,128)} reduce(f32[16384,1,2]{2,1,0:T(1,128)} %bitcast.201, f32[]{:T(128)} %broadcast.1041), dimensions={1}, to_apply=%bitcast.184.reduce_sub_computation | reduce | bytes 262148
  122.1 8.2 %reshape.611 = f32[16,1,2048]{2,1,0:T(1,128)} reshape(f32[16384,2]{1,0:T(8,128)} %reduce.114) | data formatting | bytes 262144
  130.3 8.3 %all-to-all-start = ((f32[16,1,2048]{2,1,0:T(1,128)}), f32[16,1,2048]{2,1,0:T(1,128)S(1)}, u32[]{:S(2)}, u32[]{:S(2)}) async-start(f32[16,1,2048]{2,1,0:T(1,128)} %reshape.611), calls=%async_computation.1 | async-start | bytes 262144 | tf_op jit(solution)/shard_map/all_to_all | solution.py:57
  138.9 2.8 gather_fusion
  142.0 35.5 %select_select_fusion = f32[1024]{0:T(1024)S(1)} fusion(pred[1024]{0:T(1024)(128)(4,1)S(1)} %get-tuple-element.123, pred[1024]{0:T(1024)(128)(4,1)S(1)} %get-tuple-element.124, pred[1024]{0:T(1024)(128)(4,1)S(1)} %get-tuple-element.125, pred[1024]{0:T(1024)(128)(4,1)S(1)} %get-tuple-element.126, pred[1024]{0:T(1024)(128)(4,1)S(1)} %get-tuple-element.127, ...), kind=kLoop, calls=%fused_computation.202 | loop fusion | flops 81920 | bytes 66792 | tf_op jit(solution)/shard_map/jit(_take)/select_n | solution.py:63
  177.5 1.0 reduce.115
  178.5 14.7 %reshape.612 = f32[16384,1,2]{2,1,0:T(1,128)} reshape(f32[16,2048]{1,0:T(8,128)S(1)} %reduce.115) | data formatting | bytes 262144
  193.3 5.2 %copy.267 = f32[1,2,16,1024]{3,2,1,0:T(8,128)S(1)} copy(f32[1,2,16,1024]{1,3,2,0:T(8,128)} %bitcast.202) | data formatting | bytes 262144 | tf_op jit(solution)/shard_map/all_to_all | solution.py:57
  201.2 0.6 constant_dynamic-update-slice_fusion.15
  204.2 0.6 constant_dynamic-update-slice_fusion.10
  210.8 6.9 %all-to-all-start.1 = ((bf16[16,1,2,1024]{3,2,1,0:T(2,128)(2,1)}), bf16[16,1,2,1024]{3,2,1,0:T(2,128)(2,1)S(1)}, u32[]{:S(2)}, u32[]{:S(2)}) async-start(bf16[16,1,2,1024]{3,2,1,0:T(2,128)(2,1)} %constant_dynamic-update-slice_fusion), calls=%async_computation.2 | async-start | bytes 131072 | tf_op jit(solution)/shard_map/all_to_all | solution.py:80
  217.7 7.5 %all-to-all-done.1 = bf16[16,1,2,1024]{3,2,1,0:T(2,128)(2,1)S(1)} async-done(((bf16[16,1,2,1024]{3,2,1,0:T(2,128)(2,1)}), bf16[16,1,2,1024]{3,2,1,0:T(2,128)(2,1)S(1)}, u32[]{:S(2)}, u32[]{:S(2)}) %all-to-all-start.1) | async-done | bytes 65568 | tf_op jit(solution)/shard_map/all_to_all | solution.py:80
  225.3 1.9 all_gather.3
  227.2 10.3 %convolution_convert_fusion = bf16[128,16384]{1,0:T(8,128)(2,1)} fusion(bf16[16384,512]{1,0:T(8,128)(2,1)} %param.13, bf16[1,128,512]{2,1,0:T(8,128)(2,1)S(1)} %all_gather.3), kind=kOutput, calls=%fused_computation.6 | convolution fusion | flops 2149580800 | bytes 21102592 | tf_op jit(solution)/shard_map/skm,dm->skd/dot_general | solution.py:96
  237.6 6.4 %copy.265 = bf16[128,16384]{0,1:T(8,128)(2,1)} copy(bf16[128,16384]{1,0:T(8,128)(2,1)} %convolution_convert_fusion) | data formatting | bytes 8388608 | tf_op jit(solution)/shard_map/convert_element_type | solution.py:101
  243.9 3.8 %gather_fusion.3 = bf16[512,128]{1,0:T(8,128)(2,1)S(1)} fusion(bf16[128,16384]{0,1:T(8,128)(2,1)} %copy.265, s32[1024]{0:T(1024)S(1)} %get-tuple-element.179), kind=kCustom, calls=%fused_computation.1.clone | custom fusion | bytes 264192 | tf_op jit(solution)/shard_map/jit(_take)/gather | solution.py:102
  247.9 1.0 collective-permute-start
  248.9 3.8 %gather_fusion.2 = bf16[512,128]{1,0:T(8,128)(2,1)S(1)} fusion(bf16[128,16384]{0,1:T(8,128)(2,1)} %copy.265, s32[1024]{0:T(1024)S(1)} %get-tuple-element.180), kind=kCustom, calls=%fused_computation.clone | custom fusion | bytes 264192 | tf_op jit(solution)/shard_map/jit(_take)/gather | solution.py:103
  252.8 1.3 collective-permute-start.1
  254.2 0.7 convert_element_type.61
  254.8 6.8 %scatter_custom_fusion = bf16[128,16384]{0,1:T(8,128)(2,1)} fusion(bf16[128,16384]{0,1:T(8,128)(2,1)} %copy.265, s32[512]{0:T(512)S(1)} %compare_select_fusion.14, bf16[1,128,512]{1,2,0:T(8,128)(2,1)S(1)} %collective-permute-done, f32[]{:T(128)} %constant.134.clone.1, bf16[512,128]{1,0:T(8,128)(2,1)S(1)} %gather_fusion.2, ...), kind=kCustom, calls=%fused_computation.53 | custom fusion | flops 393216 | bytes 4457472 | tf_op jit(solution)/shard_map/scatter | solution.py:114
  262.0 6.8 %scatter_custom_fusion.1 = bf16[128,16384]{0,1:T(8,128)(2,1)} fusion(bf16[128,16384]{0,1:T(8,128)(2,1)} %scatter_custom_fusion, s32[512]{0:T(512)S(1)} %compare_select_fusion.13, bf16[1,128,512]{1,2,0:T(8,128)(2,1)S(1)} %collective-permute-done.1, f32[]{:T(128)} %constant.134.clone.1, bf16[512,128]{1,0:T(8,128)(2,1)S(1)} %gather_fusion.3, ...), kind=kCustom, calls=%fused_computation.55 | custom fusion | flops 393216 | bytes 4457472 | tf_op jit(solution)/shard_map/scatter | solution.py:114
  268.8 6.4 %copy.266 = bf16[1,128,16384]{2,1,0:T(8,128)(2,1)} copy(bf16[1,128,16384]{1,2,0:T(8,128)(2,1)} %bitcast.203) | data formatting | bytes 8388608
  (92 shorter events, 14.6 us)
Async XLA Ops:
  7.2 22.3 %copy-start = (f32[8,512]{1,0:T(8,128)S(1)}, f32[8,512]{1,0:T(8,128)}, u32[]{:S(2)}) copy-start(f32[8,512]{1,0:T(8,128)} %param.16) | copy-start | bytes 49156
  7.2 11.8 %copy-start.2 = (f32[64]{0:T(128)S(1)}, f32[64]{0:T(128)}, u32[]{:S(2)}) copy-start(f32[64]{0:T(128)} %param.19) | copy-start | bytes 772
  7.2 14.7 %copy-start.5 = (s32[512]{0:T(512)S(1)}, s32[512]{0:T(512)}, u32[]{:S(2)}) copy-start(s32[512]{0:T(512)} %param.20) | copy-start | bytes 6148
  7.2 15.4 %copy-start.1 = (f32[512]{0:T(512)S(1)}, f32[512]{0:T(512)}, u32[]{:S(2)}) copy-start(f32[512]{0:T(512)} %param.18) | copy-start | bytes 6148
  7.2 26.9 %reduce-scatter.2.cloned.1.call-start = ((), (), s32[]{:S(2)}) async-start(), calls=%async_computation.3 | async-start | bytes 393216 | tf_op jit(solution)/shard_map/reduce_scatter | solution.py:44
  17.4 16.7 %copy-start.6 = (s32[512]{0:T(512)S(1)}, s32[512]{0:T(512)}, u32[]{:S(2)}) copy-start(s32[512]{0:T(512)} %param.21) | copy-start | bytes 6148
  17.4 16.7 %copy-start.3 = (f32[1,128,256]{2,1,0:T(8,128)S(1)}, f32[1,128,256]{2,1,0:T(8,128)}, u32[]{:S(2)}) copy-start(f32[1,128,256]{2,1,0:T(8,128)} %param.14) | copy-start | bytes 393220
  122.1 16.6 %copy-start.4 = (f32[16,512]{1,0:T(8,128)S(1)}, f32[16,512]{1,0:T(8,128)}, u32[]{:S(2)}) copy-start(f32[16,512]{1,0:T(8,128)} %param.17) | copy-start | bytes 98308
  130.3 47.2 %all-to-all-start = ((f32[16,1,2048]{2,1,0:T(1,128)}), f32[16,1,2048]{2,1,0:T(1,128)S(1)}, u32[]{:S(2)}, u32[]{:S(2)}) async-start(f32[16,1,2048]{2,1,0:T(1,128)} %reshape.611), calls=%async_computation.1 | async-start | bytes 262144 | tf_op jit(solution)/shard_map/all_to_all | solution.py:57
  210.8 14.4 %all-to-all-start.1 = ((bf16[16,1,2,1024]{3,2,1,0:T(2,128)(2,1)}), bf16[16,1,2,1024]{3,2,1,0:T(2,128)(2,1)S(1)}, u32[]{:S(2)}, u32[]{:S(2)}) async-start(bf16[16,1,2,1024]{3,2,1,0:T(2,128)(2,1)} %constant_dynamic-update-slice_fusion), calls=%async_computation.2 | async-start | bytes 131072 | tf_op jit(solution)/shard_map/all_to_all | solution.py:80
  247.9 7.0 %collective-permute-start = (bf16[1,128,512]{1,2,0:T(8,128)(2,1)S(1)}, bf16[1,128,512]{1,2,0:T(8,128)(2,1)S(1)}, u32[]{:S(2)}, u32[]{:S(2)}) collective-permute-start(bf16[1,128,512]{1,2,0:T(8,128)(2,1)S(1)} %bitcast_select_fusion), channel_id=1, source_target_pairs={{0,30},{2,0},{4,2},{6,4},{8,6},{10,8},{12,10},{14,12},{16,14},{18,... | collective-permute-start | bytes 393224 | tf_op jit(solution)/shard_map/ppermute | solution.py:10
  252.8 9.1 %collective-permute-start.1 = (bf16[1,128,512]{1,2,0:T(8,128)(2,1)S(1)}, bf16[1,128,512]{1,2,0:T(8,128)(2,1)S(1)}, u32[]{:S(2)}, u32[]{:S(2)}) collective-permute-start(bf16[1,128,512]{1,2,0:T(8,128)(2,1)S(1)} %bitcast_select_fusion.1), channel_id=1, source_target_pairs={{0,2},{2,4},{4,6},{6,8},{8,10},{10,12},{12,14},{14,16},{16,18},{18... | collective-permute-start | bytes 393224 | tf_op jit(solution)/shard_map/ppermute | solution.py:10
Sparse Core Ops, SparseCore 0:
  17.5 10.4 reduce-scatter.1
